TPU v7x, 32 devices: a whole 2x2x4 slice. The times are simulated.
32 devices in a mesh: ctx: 8 (over z, y), tp: 4 (over x, core).
Axes of the slice: x: 2, y: 2, z: 4, core: 2. Of those that a mesh axis runs over, the one named last changes fastest.
Arguments:
- tokens: bfloat16 [4096, 5376], P(('ctx', 'tp')), may hold values from -8 to 8
- positions: int32 [4096], replicated, may hold values from 0 to 16383, as said below
- w_query: bfloat16 [5376, 2048], P('ctx', 'tp'), may hold values from -1 to 1
- key_matrix: bfloat16 [5376, 1024], P('ctx', 'tp'), may hold values from -1 to 1
- value_matrix: bfloat16 [5376, 1024], P('ctx', 'tp'), may hold values from -0.078125 to 0.078125
- w_out: bfloat16 [2048, 5376], P('tp', 'ctx'), may hold values from -0.125 to 0.125
- gain_in: float32 [5376], replicated, may hold values from 0.1 to 1.9
- gain_query: float32 [128], replicated, may hold values from 0.5 to 14
- gain_key: float32 [128], replicated, may hold values from 0.5 to 14
- gain_post: float32 [5376], replicated, may hold values from 0.1 to 1.9
Outputs:
- layer_out: bfloat16 [4096, 5376], P(('ctx', 'tp'))
Inputs may be any that keep to these rules, and one draw needn't show every extreme that they name: (positions) rise strictly along the tokens, by 1 to 4 from one token to the next, and the last token stands at 16383.
All inputs are finite; a program needn't handle non-finite values.
Results may differ from a plain program's by a relative error of at most 0.013.
The roundings to bfloat16 on the way count: a program that leaves them out, or rounds other values in their place, can miss the bound.
Values may be sent and summed in bfloat16 or wider, within the bound.
A program may use at most 128 MiB of HBM per device.

v0:
```python
import jax
import jax.numpy as jnp
from jax import lax
from jax.sharding import PartitionSpec as P

HEAD_SIZE = 128
QS = 168
LOOKBACK_WINDOW = 1024
EPSILON = 1e-06
ROPE_BASE = 10000.0


def shifted(value, axis, steps):
    count = lax.axis_size(axis)
    leading, last = (max(0, -steps), min(count, count - steps))
    return lax.ppermute(value, axis, [(source, source + steps) for source in range(leading, last)])


def row_norm(values, scales):
    mean_square = jnp.mean(values * values, axis=-1, keepdims=True)
    return values * lax.rsqrt(mean_square + EPSILON) * scales


def rotate(head_rows, offsets):
    half_dim = head_rows.shape[-1] // 2
    frequency = ROPE_BASE ** (
        -(jnp.arange(half_dim, dtype=jnp.float32) * 2.0) / head_rows.shape[-1]
    )
    angles = offsets.astype(jnp.float32)[:, None] * frequency[None, :]
    cosine = jnp.cos(angles)[:, None, :]
    sine_wave = jnp.sin(angles)[:, None, :]
    first_half = head_rows[..., :half_dim]
    second_half = head_rows[..., half_dim:]
    return jnp.concatenate(
        [
            first_half * cosine - second_half * sine_wave,
            second_half * cosine + first_half * sine_wave,
        ],
        axis=-1,
    )


def attend(query_matrix, projected_keys, projected_values, query_offsets, key_offsets, key_valid):
    scores = jnp.einsum(
        "qkgd,skd->kgqs", query_matrix, projected_keys, preferred_element_type=jnp.float32
    ) * QS ** (-0.5)
    position_gap = query_offsets[:, None] - key_offsets[None, :]
    allowed = key_valid[None, :] & (position_gap >= 0) & (position_gap < LOOKBACK_WINDOW)
    scores = jnp.where(allowed[None, None], scores, -1e30)
    row_max = jnp.max(scores, axis=-1, keepdims=True)
    weights = jnp.where(allowed[None, None], jnp.exp(scores - row_max), 0.0)
    totals = jnp.sum(weights, axis=-1, keepdims=True)
    rounded = weights.astype(jnp.bfloat16)
    mixed = jnp.einsum(
        "kgqs,skd->qkgd", rounded, projected_values, preferred_element_type=jnp.float32
    )
    mixed = mixed / jnp.transpose(totals, (2, 0, 1, 3))
    return mixed.astype(jnp.bfloat16).reshape(query_matrix.shape[0], -1)


def shards(
    tokens,
    positions,
    w_query,
    key_matrix,
    value_matrix,
    w_out,
    gain_in,
    gain_query,
    gain_key,
    gain_post,
):
    gathered = lax.all_gather(tokens, "tp", axis=0, tiled=True)
    normalized_rows = row_norm(gathered.astype(jnp.float32), gain_in).astype(jnp.bfloat16)
    row_count = normalized_rows.shape[0]
    block_start = lax.axis_index("ctx") * row_count
    offsets_all = positions - positions[0]
    query_offsets = lax.dynamic_slice_in_dim(offsets_all, block_start, row_count, 0)

    def add_rows(weight_rows):
        return jnp.dot(normalized_rows, weight_rows, preferred_element_type=jnp.float32)

    query_raw = add_rows(lax.all_gather(w_query, "ctx", axis=0, tiled=True))
    unnormed_keys = add_rows(lax.all_gather(key_matrix, "ctx", axis=0, tiled=True))
    value_raw = add_rows(lax.all_gather(value_matrix, "ctx", axis=0, tiled=True))
    key_heads = key_matrix.shape[1] // HEAD_SIZE
    projected_keys = rotate(
        row_norm(unnormed_keys.reshape(row_count, key_heads, HEAD_SIZE), gain_key), query_offsets
    ).astype(jnp.bfloat16)
    projected_values = value_raw.astype(jnp.bfloat16).reshape(row_count, key_heads, HEAD_SIZE)
    own_pair = jnp.stack([projected_keys, projected_values])
    window_blocks = LOOKBACK_WINDOW // row_count
    earlier = []
    carried = own_pair
    for relay_step in range(window_blocks):
        carried = shifted(carried, "ctx", 1)
        earlier.insert(0, carried)
    window_pair = jnp.concatenate(earlier + [own_pair], axis=1)
    query_heads = w_query.shape[1] // HEAD_SIZE
    query_matrix = rotate(
        row_norm(query_raw.reshape(row_count, query_heads, HEAD_SIZE), gain_query), query_offsets
    ).astype(jnp.bfloat16)
    query_matrix = query_matrix.reshape(row_count, key_heads, query_heads // key_heads, HEAD_SIZE)
    padded_offsets = jnp.concatenate(
        [jnp.zeros((LOOKBACK_WINDOW,), jnp.int32), offsets_all], axis=0
    )
    key_offsets = lax.dynamic_slice_in_dim(
        padded_offsets, block_start, LOOKBACK_WINDOW + row_count, 0
    )
    key_valid = (
        block_start + jnp.arange(LOOKBACK_WINDOW + row_count, dtype=jnp.int32) >= LOOKBACK_WINDOW
    )
    attended = attend(
        query_matrix, window_pair[0], window_pair[1], query_offsets, key_offsets, key_valid
    )
    projected = jnp.dot(
        attended,
        lax.all_gather(w_out, "ctx", axis=1, tiled=True),
        preferred_element_type=jnp.float32,
    )
    summed = lax.psum_scatter(
        projected.astype(jnp.bfloat16), "tp", scatter_dimension=0, tiled=True
    ).astype(jnp.float32)
    return (tokens.astype(jnp.float32) + row_norm(summed, gain_post)).astype(jnp.bfloat16)


def solution(mesh):
    in_specs = (
        P(("ctx", "tp"), None),
        P(),
        P("ctx", "tp"),
        P("ctx", "tp"),
        P("ctx", "tp"),
        P("tp", "ctx"),
        P(),
        P(),
        P(),
        P(),
    )
    out_specs = P(("ctx", "tp"), None)
    return jax.shard_map(shards, mesh=mesh, in_specs=in_specs, out_specs=out_specs, check_vma=False)
```

profile of v0, /device:TPU:0, one launch (start us, length us, event | category | flops | bytes accessed | tf_op | source)
XLA Modules:
  0.0 434.3 jit_solution(12205699914672215212)
XLA Ops:
  6.5 0.7 all-gather.6.cloned.1.call-update
  7.3 0.7 all-gather.8.cloned.1.call-update
  8.1 0.7 all-gather.10.cloned.1.call-update
  8.8 0.5 all-gather.12.cloned.1.call-update
  9.4 0.5 all-gather.14.cloned.1.call-update
  10.0 1.2 slice.22
  11.2 1.4 broadcast_subtract_fusion
  12.6 0.5 multiply_cosine_fusion
  13.4 40.1 %all-gather.6.cloned.1.call-done = bf16[512,5376]{1,0:T(8,128)(2,1)} async-done(((bf16[128,5376]{1,0:T(8,128)(2,1)}), bf16[512,5376]{1,0:T(8,128)(2,1)}) %all-gather.6.cloned.1.call-update) | async-done | bytes 5505040 | tf_op jit(solution)/shard_map/all_gather | solution.py:73
  53.5 3.7 fusion.1
  57.3 54.5 %all-gather.8.cloned.1.call-done = bf16[5376,256]{1,0:T(8,128)(2,1)} async-done(((bf16[672,256]{1,0:T(8,128)(2,1)}), bf16[5376,256]{1,0:T(8,128)(2,1)}) %all-gather.8.cloned.1.call-update) | async-done | bytes 2752528 | tf_op jit(solution)/shard_map/all_gather | solution.py:84
  111.8 5.4 %multiply_reduce_fusion.1 = (f32[512,2]{0,1:T(2,128)S(1)}, f32[512,256]{0,1:T(8,128)S(1)}) fusion(bf16[5376,256]{1,0:T(8,128)(2,1)} %all-gather.8.cloned.1.call-done, bf16[512,5376]{1,0:T(8,128)(2,1)} %all-gather.6.cloned.1.call-done, f32[5376]{0:T(1024)S(1)} %copy-done.5, f32[512]{0:T(512)S(1)} %add_rsqrt_fusion.2), kind=kOutput, calls=%fused_computation.43 | convolution fusion | flops 1420557312 | bytes 8809472 | tf_op jit(solution)/shard_map/dot_general | solution.py:81
  117.4 51.2 %all-gather.10.cloned.1.call-done = bf16[5376,256]{1,0:T(8,128)(2,1)} async-done(((bf16[672,256]{1,0:T(8,128)(2,1)}), bf16[5376,256]{1,0:T(8,128)(2,1)}) %all-gather.10.cloned.1.call-update) | async-done | bytes 2752528 | tf_op jit(solution)/shard_map/all_gather | solution.py:85
  168.6 5.4 %convolution_convert_fusion.1 = bf16[512,256]{0,1:T(8,128)(2,1)S(1)} fusion(bf16[5376,256]{1,0:T(8,128)(2,1)} %all-gather.10.cloned.1.call-done, bf16[512,5376]{1,0:T(8,128)(2,1)} %all-gather.6.cloned.1.call-done, f32[5376]{0:T(1024)S(1)} %copy-done.5, f32[512]{0:T(512)S(1)} %add_rsqrt_fusion.2), kind=kOutput, calls=%fused_computation.30 | convolution fusion | flops 1420427264 | bytes 8543232 | tf_op jit(solution)/shard_map/dot_general | solution.py:81
  174.4 0.2 fusion.28
  174.8 2.5 collective-permute-start
  177.4 16.8 %collective-permute-done = bf16[2,512,2,128]{3,1,2,0:T(8,128)(2,1)S(1)} collective-permute-done((bf16[2,512,2,128]{3,1,2,0:T(8,128)(2,1)S(1)}, bf16[2,512,2,128]{3,1,2,0:T(8,128)(2,1)S(1)}, u32[]{:S(2)}, u32[]{:S(2)}) %collective-permute-start) | collective-permute-done | bytes 524320 | tf_op jit(solution)/shard_map/ppermute | solution.py:16
  194.2 9.1 %collective-permute-start.1 = (bf16[2,512,2,128]{3,1,2,0:T(8,128)(2,1)S(1)}, bf16[2,512,2,128]{3,1,2,0:T(8,128)(2,1)S(1)}, u32[]{:S(2)}, u32[]{:S(2)}) collective-permute-start(bf16[2,512,2,128]{3,1,2,0:T(8,128)(2,1)S(1)} %collective-permute-done), channel_id=1, source_target_pairs={{0,4},{4,8},{8,12},{12,16},{16,20},{20,24},{24,28},{1,5},{5,9},{9,... | collective-permute-start | bytes 1572872 | tf_op jit(solution)/shard_map/ppermute | solution.py:16
  203.3 1.3 fusion.11
  204.5 5.2 %collective-permute-done.1 = bf16[2,512,2,128]{3,1,2,0:T(8,128)(2,1)S(1)} collective-permute-done((bf16[2,512,2,128]{3,1,2,0:T(8,128)(2,1)S(1)}, bf16[2,512,2,128]{3,1,2,0:T(8,128)(2,1)S(1)}, u32[]{:S(2)}, u32[]{:S(2)}) %collective-permute-start.1) | collective-permute-done | bytes 524320 | tf_op jit(solution)/shard_map/ppermute | solution.py:16
  209.7 1.2 maximum_maximum_fusion
  211.0 63.6 %all-gather.12.cloned.1.call-done = bf16[5376,512]{1,0:T(8,128)(2,1)} async-done(((bf16[672,512]{1,0:T(8,128)(2,1)}), bf16[5376,512]{1,0:T(8,128)(2,1)}) %all-gather.12.cloned.1.call-update) | async-done | bytes 5505040 | tf_op jit(solution)/shard_map/all_gather | solution.py:83
  274.5 8.0 %multiply_reduce_fusion = (f32[512,4]{0,1:T(4,128)S(1)}, f32[512,512]{0,1:T(8,128)S(1)}) fusion(bf16[5376,512]{1,0:T(8,128)(2,1)} %all-gather.12.cloned.1.call-done, bf16[512,5376]{1,0:T(8,128)(2,1)} %all-gather.6.cloned.1.call-done, f32[5376]{0:T(1024)S(1)} %copy-done.5, f32[512]{0:T(512)S(1)} %add_rsqrt_fusion.2), kind=kOutput, calls=%fused_computation.32 | convolution fusion | flops 2830104576 | bytes 12090368 | tf_op jit(solution)/shard_map/dot_general | solution.py:81
  283.0 1.0 copy.23
  284.0 0.3 copy.24
  284.2 9.1 %fusion.42 = (f32[2,2,512]{2,1,0:T(2,128)S(1)}, bf16[2,2,512,1536]{2,3,1,0:T(8,128)(2,1)}) fusion(pred[512,1536]{0,1:T(8,128)(4,1)S(1)} %fusion.11, bf16[2,1536,2,128]{3,1,2,0:T(8,128)(2,1)S(1)} %maximum_maximum_fusion, bf16[512,2,2,64]{3,0,2,1:T(8,128)(2,1)S(1)} %bitcast.65, bf16[512,2,2,64]{3,0,2,1:T(8,128)(2,1)} %bitcast.64), kind=kOutput, calls=%fused_computation.63 | convolution fusion | flops 825230848 | bytes 9183232 | tf_op jit(solution)/shard_map/sub | solution.py:51
  293.3 3.9 fusion.24
  297.2 66.7 %all-gather.14.cloned.1.call-done = bf16[512,5376]{0,1:T(8,128)(2,1)} async-done(((bf16[512,672]{0,1:T(8,128)(2,1)}), bf16[512,5376]{0,1:T(8,128)(2,1)}) %all-gather.14.cloned.1.call-update) | async-done | bytes 5505040 | tf_op jit(solution)/shard_map/all_gather | solution.py:118
  363.9 7.5 %convolution_convert_fusion = bf16[512,5376]{1,0:T(8,128)(2,1)} fusion(bf16[512,512]{0,1:T(8,128)(2,1)S(1)} %bitcast.68, bf16[512,5376]{0,1:T(8,128)(2,1)} %all-gather.14.cloned.1.call-done), kind=kOutput, calls=%fused_computation.9 | convolution fusion | flops 2821324800 | bytes 11534336 | tf_op jit(solution)/shard_map/dot_general | solution.py:116
  371.4 51.3 %reduce-scatter.2.cloned.1.call-done = bf16[128,5376]{1,0:T(8,128)(2,1)} async-done(((bf16[512,5376]{1,0:T(8,128)(2,1)}), bf16[128,5376]{1,0:T(8,128)(2,1)}) %reduce-scatter.2.cloned.1.call-update) | async-done | bytes 1376272 | tf_op jit(solution)/shard_map/reduce_scatter | solution.py:121
  422.7 1.7 fusion.12
  424.4 3.0 fusion.15
  (35 shorter events, 1.8 us)
Async XLA Ops:
  6.5 105.2 %copy-start.5 = (f32[5376]{0:T(1024)S(1)}, f32[5376]{0:T(1024)}, u32[]{:S(2)}) copy-start(f32[5376]{0:T(1024)} %param.16) | copy-start | bytes 64516
  6.5 47.0 %all-gather.6.cloned.1.call-start = ((), (), s32[]{:S(2)}) async-start(), calls=%async_computation.1 | async-start | bytes 6881280 | tf_op jit(solution)/shard_map/all_gather | solution.py:73
  7.3 104.5 %all-gather.8.cloned.1.call-start = ((), (), s32[]{:S(2)}) async-start(), calls=%async_computation.2 | async-start | bytes 3096576 | tf_op jit(solution)/shard_map/all_gather | solution.py:84
  8.0 160.6 %all-gather.10.cloned.1.call-start = ((), (), s32[]{:S(2)}) async-start(), calls=%async_computation.3 | async-start | bytes 3096576 | tf_op jit(solution)/shard_map/all_gather | solution.py:85
  8.7 265.8 %all-gather.12.cloned.1.call-start = ((), (), s32[]{:S(2)}) async-start(), calls=%async_computation.4 | async-start | bytes 6193152 | tf_op jit(solution)/shard_map/all_gather | solution.py:83
  9.3 354.5 %all-gather.14.cloned.1.call-start = ((), (), s32[]{:S(2)}) async-start(), calls=%async_computation.5 | async-start | bytes 6193152 | tf_op jit(solution)/shard_map/all_gather | solution.py:118
  9.9 412.8 %reduce-scatter.2.cloned.1.call-start = ((), (), s32[]{:S(2)}) async-start(), calls=%async_computation.6 | async-start | bytes 6881280 | tf_op jit(solution)/shard_map/reduce_scatter | solution.py:121
  117.4 56.8 %copy-start.3 = (f32[128]{0:T(128)S(1)}, f32[128]{0:T(128)}, u32[]{:S(2)}) copy-start(f32[128]{0:T(128)} %param.18) | copy-start | bytes 1540
  174.8 19.4 %collective-permute-start = (bf16[2,512,2,128]{3,1,2,0:T(8,128)(2,1)S(1)}, bf16[2,512,2,128]{3,1,2,0:T(8,128)(2,1)S(1)}, u32[]{:S(2)}, u32[]{:S(2)}) collective-permute-start(bf16[2,512,2,128]{3,1,2,0:T(8,128)(2,1)S(1)} %pad_maximum_fusion), channel_id=1, source_target_pairs={{0,4},{4,8},{8,12},{12,16},{16,20},{20,24},{24,28},{1,5},{5,9},{9,... | collective-permute-start | bytes 1572872 | tf_op jit(solution)/shard_map/ppermute | solution.py:16
  194.2 10.4 %copy-start.1 = (bf16[2,512,2,128]{3,1,2,0:T(8,128)(2,1)}, bf16[2,512,2,128]{3,1,2,0:T(8,128)(2,1)S(1)}, u32[]{:S(2)}) copy-start(bf16[2,512,2,128]{3,1,2,0:T(8,128)(2,1)S(1)} %collective-permute-done) | copy-start | bytes 1572868
  194.2 15.5 %collective-permute-start.1 = (bf16[2,512,2,128]{3,1,2,0:T(8,128)(2,1)S(1)}, bf16[2,512,2,128]{3,1,2,0:T(8,128)(2,1)S(1)}, u32[]{:S(2)}, u32[]{:S(2)}) collective-permute-start(bf16[2,512,2,128]{3,1,2,0:T(8,128)(2,1)S(1)} %collective-permute-done), channel_id=1, source_target_pairs={{0,4},{4,8},{8,12},{12,16},{16,20},{20,24},{24,28},{1,5},{5,9},{9,... | collective-permute-start | bytes 1572872 | tf_op jit(solution)/shard_map/ppermute | solution.py:16
  211.0 71.6 %copy-start.4 = (f32[128]{0:T(128)S(1)}, f32[128]{0:T(128)}, u32[]{:S(2)}) copy-start(f32[128]{0:T(128)} %param.17) | copy-start | bytes 1540
  371.4 53.0 %copy-start = (bf16[128,5376]{1,0:T(8,128)(2,1)S(1)}, bf16[128,5376]{1,0:T(8,128)(2,1)}, u32[]{:S(2)}) copy-start(bf16[128,5376]{1,0:T(8,128)(2,1)} %param.10) | copy-start | bytes 4128772
  371.4 53.1 %copy-start.2 = (f32[5376]{0:T(1024)S(1)}, f32[5376]{0:T(1024)}, u32[]{:S(2)}) copy-start(f32[5376]{0:T(1024)} %param.19) | copy-start | bytes 64516
Sparse Core Ops, SparseCore 0:
  8.9 44.6 all-gather.5
  55.7 55.9 all-gather.7
  114.0 54.5 all-gather.9
  170.6 103.8 all-gather.11
  276.6 87.2 all-gather.13
  371.5 51.1 reduce-scatter.1
where the time goes:
time: 435 us; the launch traced here: 434 us
  waiting for transfers between devices  353 us (81%)
  matrix products  39.2 us (9%)
  other arithmetic  13.9 us (3%)
  between operations  13.7 us (3%)
  starting transfers between devices  11.8 us (3%)
    all_gather x1, waiting for transfers between devices, shards(): lax.all_gather(w_out, 'ctx', axis=1, tiled=True)  66.7 us
    all_gather x1, waiting for transfers between devices, shards(): query_raw = add_rows(lax.all_gather(w_query, 'ctx', axis=0, tiled=True))  63.6 us
    all_gather x1, waiting for transfers between devices, shards(): lax.all_gather(key_matrix, 'ctx', axis=0, tiled=True)  54.5 us
    reduce_scatter x1, waiting for transfers between devices, shards(): lax.psum_scatter(projected.astype(jnp.bfloat16), 'tp', scatter_dimension=...  51.3 us
    all_gather x1, waiting for transfers between devices, shards(): lax.all_gather(value_matrix, 'ctx', axis=0, tiled=True)  51.2 us
    all_gather x1, waiting for transfers between devices, shards(): gathered = lax.all_gather(tokens, 'tp', axis=0, tiled=True)  40.1 us
    ppermute x2, waiting for transfers between devices, shifted(): lax.ppermute(value, axis, [(source, source + steps) for source in range(l...  22 us
    dot_general x3, matrix products, add_rows(): jnp.dot(normalized_rows, weight_rows, preferred_element_type=jnp.float32)  18.8 us
  transfers between devices with their start and end apart: 8, of which 8 were waited for; matrix products, arithmetic and copies ran while one was open for 10% of the time, Pallas kernels for 0%

commit v1 on v0

--- a/solution.py
+++ b/solution.py
@@ -8,6 +8,13 @@
 LOOKBACK_WINDOW = 1024
 EPSILON = 1e-06
 ROPE_BASE = 10000.0
+
+
+def swapped_in(x, name, dim):
+    size = lax.axis_size(name)
+    blocks = jnp.stack([x for _ in range(size)])
+    blocks = lax.all_to_all(blocks, name, split_axis=0, concat_axis=0)
+    return jnp.concatenate(blocks, axis=dim)
 
 
 def shifted(value, axis, steps):
@@ -80,7 +87,7 @@
     def add_rows(weight_rows):
         return jnp.dot(normalized_rows, weight_rows, preferred_element_type=jnp.float32)
 
-    query_raw = add_rows(lax.all_gather(w_query, "ctx", axis=0, tiled=True))
+    query_raw = add_rows(swapped_in(w_query, "ctx", 0))
     unnormed_keys = add_rows(lax.all_gather(key_matrix, "ctx", axis=0, tiled=True))
     value_raw = add_rows(lax.all_gather(value_matrix, "ctx", axis=0, tiled=True))
     key_heads = key_matrix.shape[1] // HEAD_SIZE

time: 435 us -> 410 us (0.943)
  waiting for transfers between devices: 353 us -> 311 us
  local copies, waits for them, and re-layouts: 3.21 us -> 14.8 us
  starting transfers between devices: 11.8 us -> 19.1 us
    all_gather x1, waiting for transfers between devices: 54.5 us -> 119 us  [shards(): lax.all_gather(key_matrix, 'ctx', axis=0, tiled=True)]
    all_gather x1 -> x0, waiting for transfers between devices: 63.6 us -> none  [shards(): query_raw = add_rows(lax.all_gather(w_query, 'ctx', axis=0, tiled=True))]
    all_gather x1, waiting for transfers between devices: 66.7 us -> 33.8 us  [shards(): lax.all_gather(w_out, 'ctx', axis=1, tiled=True)]
    all_gather x1, waiting for transfers between devices: 40.1 us -> 30.7 us  [shards(): gathered = lax.all_gather(tokens, 'tp', axis=0, tiled=True)]
    dot_general x0 -> x1, local copies, waits for them, and re-layouts: none -> 8.31 us  [add_rows(): jnp.dot(normalized_rows, weight_rows, preferred_element_type=jnp.float32)]
    all_to_all x0 -> x1, starting transfers between devices: none -> 7.44 us  [swapped_in(): blocks = lax.all_to_all(blocks, name, split_axis=0, concat_axis=0)]
  transfers between devices with their start and end apart: 8 -> 8, of which waited for: 8 -> 7; matrix products, arithmetic and copies ran while one was open for 10% -> 13% of each run, Pallas kernels for 0% -> 0%
where the time goes in v1:
time: 410 us; the launch traced here: 409 us
  waiting for transfers between devices  311 us (76%)
  matrix products  38 us (9%)
  starting transfers between devices  19.1 us (5%)
  local copies, waits for them, and re-layouts  14.8 us (4%)
  between operations  13.4 us (3%)
  other arithmetic  13.2 us (3%)
    all_gather x1, waiting for transfers between devices, shards(): lax.all_gather(key_matrix, 'ctx', axis=0, tiled=True)  119 us
    reduce_scatter x1, waiting for transfers between devices, shards(): lax.psum_scatter(projected.astype(jnp.bfloat16), 'tp', scatter_dimension=...  51.3 us
    all_gather x1, waiting for transfers between devices, shards(): lax.all_gather(value_matrix, 'ctx', axis=0, tiled=True)  50.9 us
    all_gather x1, waiting for transfers between devices, shards(): lax.all_gather(w_out, 'ctx', axis=1, tiled=True)  33.8 us
    all_gather x1, waiting for transfers between devices, shards(): gathered = lax.all_gather(tokens, 'tp', axis=0, tiled=True)  30.7 us
    ppermute x2, waiting for transfers between devices, shifted(): lax.ppermute(value, axis, [(source, source + steps) for source in range(l...  22 us
    dot_general x3, matrix products, add_rows(): jnp.dot(normalized_rows, weight_rows, preferred_element_type=jnp.float32)  17.6 us
    ppermute x2, starting transfers between devices, shifted(): lax.ppermute(value, axis, [(source, source + steps) for source in range(l...  11.5 us
  transfers between devices with their start and end apart: 8, of which 7 were waited for; matrix products, arithmetic and copies ran while one was open for 13% of the time, Pallas kernels for 0%

profile of v1, /device:TPU:0, one launch (start us, length us, event | category | flops | bytes accessed | tf_op | source)
XLA Modules:
  0.0 409.2 jit_solution(415485943000765825)
XLA Ops:
  6.5 0.7 all-gather.5.cloned.1.call-update
  7.3 0.7 all-gather.7.cloned.1.call-update
  8.1 0.7 all-gather.9.cloned.1.call-update
  8.7 4.0 stack.5
  12.7 7.4 %all-to-all-start = ((bf16[8,672,512]{2,1,0:T(8,128)(2,1)}), bf16[8,672,512]{2,1,0:T(8,128)(2,1)}, u32[]{:S(2)}, u32[]{:S(2)}) async-start(bf16[8,672,512]{2,1,0:T(8,128)(2,1)} %stack.5), calls=%async_computation | async-start | bytes 11010048 | tf_op jit(solution)/shard_map/all_to_all | solution.py:16
  20.2 0.5 all-gather.11.cloned.1.call-update
  20.8 0.5 slice.22
  21.3 0.7 broadcast_subtract_fusion
  22.1 0.5 multiply_cosine_fusion
  22.9 30.7 %all-gather.5.cloned.1.call-done = bf16[512,5376]{1,0:T(8,128)(2,1)} async-done(((bf16[128,5376]{1,0:T(8,128)(2,1)}), bf16[512,5376]{1,0:T(8,128)(2,1)}) %all-gather.5.cloned.1.call-update) | async-done | bytes 5505040 | tf_op jit(solution)/shard_map/all_gather | solution.py:80
  53.5 3.7 fusion.1
  57.3 119.4 %all-gather.7.cloned.1.call-done = bf16[5376,256]{1,0:T(8,128)(2,1)} async-done(((bf16[672,256]{1,0:T(8,128)(2,1)}), bf16[5376,256]{1,0:T(8,128)(2,1)}) %all-gather.7.cloned.1.call-update) | async-done | bytes 2752528 | tf_op jit(solution)/shard_map/all_gather | solution.py:91
  176.7 5.4 %multiply_reduce_fusion.1 = (f32[512,2]{0,1:T(2,128)S(1)}, f32[512,256]{0,1:T(8,128)S(1)}) fusion(bf16[5376,256]{1,0:T(8,128)(2,1)} %all-gather.7.cloned.1.call-done, bf16[512,5376]{1,0:T(8,128)(2,1)} %all-gather.5.cloned.1.call-done, f32[5376]{0:T(1024)S(1)} %copy-done.6, f32[512]{0:T(512)S(1)} %add_rsqrt_fusion.2), kind=kOutput, calls=%fused_computation.45 | convolution fusion | flops 1420557312 | bytes 8809472 | tf_op jit(solution)/shard_map/dot_general | solution.py:88
  182.3 50.9 %all-gather.9.cloned.1.call-done = bf16[5376,256]{1,0:T(8,128)(2,1)} async-done(((bf16[672,256]{1,0:T(8,128)(2,1)}), bf16[5376,256]{1,0:T(8,128)(2,1)}) %all-gather.9.cloned.1.call-update) | async-done | bytes 2752528 | tf_op jit(solution)/shard_map/all_gather | solution.py:92
  233.2 5.4 %convolution_convert_fusion.1 = bf16[512,256]{0,1:T(8,128)(2,1)S(1)} fusion(bf16[5376,256]{1,0:T(8,128)(2,1)} %all-gather.9.cloned.1.call-done, bf16[512,5376]{1,0:T(8,128)(2,1)} %all-gather.5.cloned.1.call-done, f32[5376]{0:T(1024)S(1)} %copy-done.6, f32[512]{0:T(512)S(1)} %add_rsqrt_fusion.2), kind=kOutput, calls=%fused_computation.32 | convolution fusion | flops 1420427264 | bytes 8543232 | tf_op jit(solution)/shard_map/dot_general | solution.py:88
  239.4 2.5 collective-permute-start
  242.0 16.8 %collective-permute-done = bf16[2,512,2,128]{3,1,2,0:T(8,128)(2,1)S(1)} collective-permute-done((bf16[2,512,2,128]{3,1,2,0:T(8,128)(2,1)S(1)}, bf16[2,512,2,128]{3,1,2,0:T(8,128)(2,1)S(1)}, u32[]{:S(2)}, u32[]{:S(2)}) %collective-permute-start) | collective-permute-done | bytes 524320 | tf_op jit(solution)/shard_map/ppermute | solution.py:23
  258.8 9.0 %collective-permute-start.1 = (bf16[2,512,2,128]{3,1,2,0:T(8,128)(2,1)S(1)}, bf16[2,512,2,128]{3,1,2,0:T(8,128)(2,1)S(1)}, u32[]{:S(2)}, u32[]{:S(2)}) collective-permute-start(bf16[2,512,2,128]{3,1,2,0:T(8,128)(2,1)S(1)} %collective-permute-done), channel_id=1, source_target_pairs={{0,4},{4,8},{8,12},{12,16},{16,20},{20,24},{24,28},{1,5},{5,9},{9,... | collective-permute-start | bytes 1572872 | tf_op jit(solution)/shard_map/ppermute | solution.py:23
  267.9 1.3 fusion.13
  269.1 5.2 %collective-permute-done.1 = bf16[2,512,2,128]{3,1,2,0:T(8,128)(2,1)S(1)} collective-permute-done((bf16[2,512,2,128]{3,1,2,0:T(8,128)(2,1)S(1)}, bf16[2,512,2,128]{3,1,2,0:T(8,128)(2,1)S(1)}, u32[]{:S(2)}, u32[]{:S(2)}) %collective-permute-start.1) | collective-permute-done | bytes 524320 | tf_op jit(solution)/shard_map/ppermute | solution.py:23
  274.3 1.2 maximum_maximum_fusion
  275.6 8.3 %copy.24 = bf16[512,5376]{1,0:T(8,128)(2,1)} copy(bf16[512,5376]{0,1:T(8,128)(2,1)} %bitcast.12) | data formatting | bytes 11010048 | tf_op jit(solution)/shard_map/dot_general | solution.py:88
  283.9 6.9 %multiply_reduce_fusion = (f32[512,4]{0,1:T(4,128)S(1)}, f32[512,4,128]{0,2,1:T(8,128)S(1)}) fusion(bf16[4,128,5376]{2,1,0:T(8,128)(2,1)} %bitcast.70, f32[5376]{0:T(1024)S(1)} %copy-done.6, f32[512]{0:T(512)S(1)} %add_rsqrt_fusion.2, bf16[512,5376]{1,0:T(8,128)(2,1)} %all-gather.5.cloned.1.call-done), kind=kOutput, calls=%fused_computation.34 | convolution fusion | flops 2830104576 | bytes 12090368 | tf_op jit(solution)/shard_map/dot_general | solution.py:88
  291.2 1.0 copy.25
  292.2 0.3 copy.26
  292.5 9.0 %fusion.43 = (f32[2,2,512]{2,1,0:T(2,128)S(1)}, bf16[2,2,512,1536]{2,3,1,0:T(8,128)(2,1)}) fusion(pred[512,1536]{0,1:T(8,128)(4,1)S(1)} %fusion.13, bf16[2,1536,2,128]{3,1,2,0:T(8,128)(2,1)S(1)} %maximum_maximum_fusion, bf16[512,2,2,64]{3,0,2,1:T(8,128)(2,1)S(1)} %copy.26, bf16[512,2,2,64]{3,0,2,1:T(8,128)(2,1)} %copy.25), kind=kOutput, calls=%fused_computation.64 | convolution fusion | flops 825230848 | bytes 9183232 | tf_op jit(solution)/shard_map/sub | solution.py:58
  301.5 3.8 fusion.26
  305.3 33.8 %all-gather.11.cloned.1.call-done = bf16[512,5376]{0,1:T(8,128)(2,1)} async-done(((bf16[512,672]{0,1:T(8,128)(2,1)}), bf16[512,5376]{0,1:T(8,128)(2,1)}) %all-gather.11.cloned.1.call-update) | async-done | bytes 5505040 | tf_op jit(solution)/shard_map/all_gather | solution.py:125
  339.1 7.5 %convolution_convert_fusion = bf16[512,5376]{1,0:T(8,128)(2,1)} fusion(bf16[512,512]{0,1:T(8,128)(2,1)S(1)} %bitcast.75, bf16[512,5376]{0,1:T(8,128)(2,1)} %all-gather.11.cloned.1.call-done), kind=kOutput, calls=%fused_computation.9 | convolution fusion | flops 2821324800 | bytes 11534336 | tf_op jit(solution)/shard_map/dot_general | solution.py:123
  346.7 51.3 %reduce-scatter.2.cloned.1.call-done = bf16[128,5376]{1,0:T(8,128)(2,1)} async-done(((bf16[512,5376]{1,0:T(8,128)(2,1)}), bf16[128,5376]{1,0:T(8,128)(2,1)}) %reduce-scatter.2.cloned.1.call-update) | async-done | bytes 1376272 | tf_op jit(solution)/shard_map/reduce_scatter | solution.py:128
  398.0 1.7 fusion.14
  399.7 3.0 fusion.17
  (38 shorter events, 2.0 us)
Async XLA Ops:
  6.5 47.0 %all-gather.5.cloned.1.call-start = ((), (), s32[]{:S(2)}) async-start(), calls=%async_computation.2 | async-start | bytes 6881280 | tf_op jit(solution)/shard_map/all_gather | solution.py:80
  7.3 169.4 %all-gather.7.cloned.1.call-start = ((), (), s32[]{:S(2)}) async-start(), calls=%async_computation.3 | async-start | bytes 3096576 | tf_op jit(solution)/shard_map/all_gather | solution.py:91
  8.0 225.2 %all-gather.9.cloned.1.call-start = ((), (), s32[]{:S(2)}) async-start(), calls=%async_computation.4 | async-start | bytes 3096576 | tf_op jit(solution)/shard_map/all_gather | solution.py:92
  12.7 8.1 %copy-start.3 = (s32[4096]{0:T(1024)S(1)}, s32[4096]{0:T(1024)}, u32[]{:S(2)}) copy-start(s32[4096]{0:T(1024)} %param.11) | copy-start | bytes 49156
  12.7 262.9 %all-to-all-start = ((bf16[8,672,512]{2,1,0:T(8,128)(2,1)}), bf16[8,672,512]{2,1,0:T(8,128)(2,1)}, u32[]{:S(2)}, u32[]{:S(2)}) async-start(bf16[8,672,512]{2,1,0:T(8,128)(2,1)} %stack.5), calls=%async_computation | async-start | bytes 11010048 | tf_op jit(solution)/shard_map/all_to_all | solution.py:16
  20.1 156.5 %copy-start.6 = (f32[5376]{0:T(1024)S(1)}, f32[5376]{0:T(1024)}, u32[]{:S(2)}) copy-start(f32[5376]{0:T(1024)} %param.16) | copy-start | bytes 64516
  20.1 319.0 %all-gather.11.cloned.1.call-start = ((), (), s32[]{:S(2)}) async-start(), calls=%async_computation.5 | async-start | bytes 6193152 | tf_op jit(solution)/shard_map/all_gather | solution.py:125
  20.7 377.3 %reduce-scatter.2.cloned.1.call-start = ((), (), s32[]{:S(2)}) async-start(), calls=%async_computation.6 | async-start | bytes 6881280 | tf_op jit(solution)/shard_map/reduce_scatter | solution.py:128
  182.3 56.5 %copy-start.4 = (f32[128]{0:T(128)S(1)}, f32[128]{0:T(128)}, u32[]{:S(2)}) copy-start(f32[128]{0:T(128)} %param.18) | copy-start | bytes 1540
  239.4 19.4 %collective-permute-start = (bf16[2,512,2,128]{3,1,2,0:T(8,128)(2,1)S(1)}, bf16[2,512,2,128]{3,1,2,0:T(8,128)(2,1)S(1)}, u32[]{:S(2)}, u32[]{:S(2)}) collective-permute-start(bf16[2,512,2,128]{3,1,2,0:T(8,128)(2,1)S(1)} %pad_maximum_fusion), channel_id=1, source_target_pairs={{0,4},{4,8},{8,12},{12,16},{16,20},{20,24},{24,28},{1,5},{5,9},{9,... | collective-permute-start | bytes 1572872 | tf_op jit(solution)/shard_map/ppermute | solution.py:23
  258.8 10.3 %copy-start.1 = (bf16[2,512,2,128]{3,1,2,0:T(8,128)(2,1)}, bf16[2,512,2,128]{3,1,2,0:T(8,128)(2,1)S(1)}, u32[]{:S(2)}) copy-start(bf16[2,512,2,128]{3,1,2,0:T(8,128)(2,1)S(1)} %collective-permute-done) | copy-start | bytes 1572868
  258.8 15.5 %collective-permute-start.1 = (bf16[2,512,2,128]{3,1,2,0:T(8,128)(2,1)S(1)}, bf16[2,512,2,128]{3,1,2,0:T(8,128)(2,1)S(1)}, u32[]{:S(2)}, u32[]{:S(2)}) collective-permute-start(bf16[2,512,2,128]{3,1,2,0:T(8,128)(2,1)S(1)} %collective-permute-done), channel_id=1, source_target_pairs={{0,4},{4,8},{8,12},{12,16},{16,20},{20,24},{24,28},{1,5},{5,9},{9,... | collective-permute-start | bytes 1572872 | tf_op jit(solution)/shard_map/ppermute | solution.py:23
  283.9 6.9 %copy-start.5 = (f32[128]{0:T(128)S(1)}, f32[128]{0:T(128)}, u32[]{:S(2)}) copy-start(f32[128]{0:T(128)} %param.17) | copy-start | bytes 1540
  346.6 53.0 %copy-start = (bf16[128,5376]{1,0:T(8,128)(2,1)S(1)}, bf16[128,5376]{1,0:T(8,128)(2,1)}, u32[]{:S(2)}) copy-start(bf16[128,5376]{1,0:T(8,128)(2,1)} %param.10) | copy-start | bytes 4128772
  346.6 53.1 %copy-start.2 = (f32[5376]{0:T(1024)S(1)}, f32[5376]{0:T(1024)}, u32[]{:S(2)}) copy-start(f32[5376]{0:T(1024)} %param.19) | copy-start | bytes 64516
Sparse Core Ops, SparseCore 0:
  8.9 44.6 all-gather.4
  55.7 120.9 all-gather.6
  178.9 54.2 all-gather.8
  235.2 103.8 all-gather.10
  346.8 51.1 reduce-scatter.1
